TPU v7x, 32 devices: a whole 2x2x4 slice. The times are simulated.
32 devices in a mesh: groups: 2 (over x), seq: 16 (over z, y, core).
Axes of the slice: x: 2, y: 2, z: 4, core: 2. Of those that a mesh axis runs over, the one named last changes fastest.
Arguments:
- queries: bfloat16 [4096, 8192], P(('groups', 'seq')), parts along dimension 0, may hold values from -4.5 to 4.5
- keyvalue: bfloat16 [4096, 2048], P(('groups', 'seq')), parts along dimension 0, may hold values from -4.5 to 4.5
- doc_ids: int32 [4096], P(('groups', 'seq')), parts along dimension 0, may hold values from 0 to 7, never falling along the last dimension, each value on 1 to 512 neighbouring positions
- owner_tiles: int32 [32, 2], P(('groups', 'seq')), parts along dimension 0, may hold values from 0 to 15, as said below
- tile_counts: int32 [32], P(('groups', 'seq')), parts along dimension 0, may hold values from 0 to 2, as said below
Outputs:
- owned: bfloat16 [8192, 8192], P(('groups', 'seq')), parts along dimension 0
There are 2 independent parts, one for each index of `groups`. A program takes and returns all parts, laid end to end along the dimension named above; each array names one. Nothing has to cross between parts.
Inputs may be any that keep to these rules, and one draw needn't show every extreme that they name: `owner_tiles`: over the slots below each owner's count, every tile 0 to 15 is listed exactly once; the other slots hold 0. Tile t is listed either by its holder, the owner o with o * 128 <= t * 128 < (o + 1) * 128, or by the holder's partner, the owner whose index differs from the holder's by half the number of owners. `tile_counts`: the counts sum to 16; each is 0, 1 or 2, some owner has 2, and an owner has 2 exactly when its partner has 0.
All inputs are finite; a program needn't handle non-finite values.
Results may differ from a plain program's by a relative error of at most 0.0034.
Values may be sent and summed in bfloat16 or wider, within the bound.
A program may use at most 64 MiB of HBM per device.

v0:
```python
import jax
import jax.numpy as jnp
from jax import lax
from jax.sharding import PartitionSpec as P

QUERY_HEADS = 64
KEY_VALUE_HEADS = 8
HEAD_WIDTH = 128
TILE = 128
DOCUMENT_LIMIT = 512


def from_behind(shard, axis, by):
    count = lax.axis_size(axis)
    pairs = [(i, i + by) for i in range(count) if 0 <= i + by < count]
    return lax.ppermute(shard, axis, pairs)


def attend(queries, keys, value_rows, allowed):
    scale = queries.shape[-1] ** (-0.5)
    scores = jnp.einsum("rhgd,khd->hgrk", queries, keys, preferred_element_type=jnp.float32) * scale
    scores = jnp.where(allowed[None, None], scores, -jnp.inf)
    row_top = jnp.max(scores, axis=3, keepdims=True)
    exponent = jnp.exp(scores - row_top)
    totals = jnp.sum(exponent, axis=3, keepdims=True)
    weights = exponent.astype(jnp.bfloat16)
    mixed_rows = jnp.einsum(
        "hgrk,khd->rhgd", weights, value_rows, preferred_element_type=jnp.float32
    )
    return (mixed_rows / jnp.transpose(totals, (2, 0, 1, 3))).astype(jnp.bfloat16)


def deliver_owners(head_rows, all_lists, owner_tiles, seq_count, width):
    slots_dev = owner_tiles.shape[1]
    slot_rows = slots_dev * TILE
    tile_rows = jnp.arange(TILE, dtype=jnp.int32)
    row_index = jnp.transpose(all_lists)[:, None, :] * TILE + tile_rows[None, :, None]
    send_rows = jnp.take(head_rows, row_index.reshape(slot_rows, seq_count), axis=0)
    received = lax.all_to_all(send_rows, "seq", split_axis=1, concat_axis=1, tiled=True)
    return received.reshape(slot_rows, width)


def local(queries, keyvalue, doc_ids, owner_tiles, tile_counts):
    seq_count = lax.axis_size("seq")
    token_per_holder = queries.shape[0]
    width = queries.shape[1]
    head_share = QUERY_HEADS // seq_count
    group_width = QUERY_HEADS // KEY_VALUE_HEADS
    head_cols = head_share * HEAD_WIDTH
    slots_dev = owner_tiles.shape[1]
    reach_devs = (DOCUMENT_LIMIT - 1) // token_per_holder + 1
    doc_marks = doc_ids + 1
    kv_parts = [keyvalue]
    mark_parts = [doc_marks]
    for shift_by in range(1, reach_devs + 1):
        far_kv, far_marks = from_behind((keyvalue, doc_marks), "seq", shift_by)
        kv_parts.insert(0, far_kv)
        mark_parts.insert(0, far_marks)
    kv_near = jnp.concatenate(kv_parts, axis=0)
    near_marks = jnp.concatenate(mark_parts, axis=0)
    near_rows = kv_near.shape[0]
    keyvalue_grouped = kv_near.reshape(near_rows, KEY_VALUE_HEADS, 2, HEAD_WIDTH)
    q_place = jnp.arange(token_per_holder, dtype=jnp.int32) + reach_devs * token_per_holder
    k_place = jnp.arange(near_rows, dtype=jnp.int32)
    allowed = (doc_marks[:, None] == near_marks[None, :]) & (k_place[None, :] <= q_place[:, None])
    local_out = attend(
        queries.reshape(token_per_holder, KEY_VALUE_HEADS, group_width, HEAD_WIDTH),
        keyvalue_grouped[:, :, 0],
        keyvalue_grouped[:, :, 1],
        allowed,
    )
    local_out = local_out.reshape(token_per_holder, width)
    all_lists = lax.all_gather(owner_tiles, "seq", axis=0, tiled=True)
    out_send = local_out.reshape(token_per_holder, seq_count, head_cols)
    head_rows = lax.all_to_all(out_send, "seq", split_axis=1, concat_axis=0, tiled=True).reshape(
        token_per_holder * seq_count, head_cols
    )
    owned = deliver_owners(head_rows, all_lists, owner_tiles, seq_count, width)
    live = jnp.repeat(jnp.arange(slots_dev, dtype=jnp.int32) < tile_counts[0], TILE)
    return jnp.where(live[:, None], owned, jnp.zeros((), jnp.bfloat16))


def solution(mesh):
    placed = (
        P(("groups", "seq"), None),
        P(("groups", "seq"), None),
        P(("groups", "seq")),
        P(("groups", "seq"), None),
        P(("groups", "seq")),
    )
    return jax.shard_map(
        local, mesh=mesh, in_specs=placed, out_specs=P(("groups", "seq"), None), check_vma=False
    )
```

profile of v0, /device:TPU:15, one launch (start us, length us, event | category | flops | bytes accessed | tf_op | source)
XLA Modules:
  0.0 285.1 jit_solution(12777522837619255446)
XLA Ops:
  0.0 0.7 broadcast_add_fusion
  0.7 3.2 %collective-permute-start.4 = (s32[128]{0:T(128)S(1)}, s32[128]{0:T(128)S(1)}, u32[]{:S(2)}, u32[]{:S(2)}) collective-permute-start(s32[128]{0:T(128)S(1)} %broadcast_add_fusion), channel_id=1, source_target_pairs={{0,4},{1,5},{2,6},{3,7},{4,8},{5,9},{6,10},{7,11},{8,12},{9,13},{1... | collective-permute-start | bytes 1544 | tf_op jit(solution)/shard_map/ppermute | solution.py:16
  3.9 4.0 %collective-permute-start.5 = (s32[128]{0:T(128)S(1)}, s32[128]{0:T(128)S(1)}, u32[]{:S(2)}, u32[]{:S(2)}) collective-permute-start(s32[128]{0:T(128)S(1)} %broadcast_add_fusion), channel_id=1, source_target_pairs={{0,3},{1,4},{2,5},{3,6},{4,7},{5,8},{6,9},{7,10},{8,11},{9,12},{10... | collective-permute-start | bytes 1544 | tf_op jit(solution)/shard_map/ppermute | solution.py:16
  8.0 1.9 collective-permute-start.6
  9.9 3.4 %collective-permute-start.7 = (s32[128]{0:T(128)S(1)}, s32[128]{0:T(128)S(1)}, u32[]{:S(2)}, u32[]{:S(2)}) collective-permute-start(s32[128]{0:T(128)S(1)} %broadcast_add_fusion), channel_id=1, source_target_pairs={{0,1},{1,2},{2,3},{3,4},{4,5},{5,6},{6,7},{7,8},{8,9},{9,10},{10,1... | collective-permute-start | bytes 1544 | tf_op jit(solution)/shard_map/ppermute | solution.py:16
  13.3 1.3 copy.52
  14.6 1.9 collective-permute-start
  16.6 2.2 copy.71
  18.8 0.0 collective-permute-done.4
  18.8 1.9 collective-permute-start.1
  20.7 0.0 collective-permute-done.5
  20.7 1.9 collective-permute-start.2
  22.7 0.0 collective-permute-done.6
  22.7 2.2 collective-permute-start.3
  24.9 0.0 collective-permute-done.7
  24.9 0.2 fusion.11
  25.1 5.3 %collective-permute-done = bf16[128,2048]{0,1:T(8,128)(2,1)S(1)} collective-permute-done((bf16[128,2048]{0,1:T(8,128)(2,1)S(1)}, bf16[128,2048]{0,1:T(8,128)(2,1)S(1)}, u32[]{:S(2)}, u32[]{:S(2)}) %collective-permute-start) | collective-permute-done | bytes 524320 | tf_op jit(solution)/shard_map/ppermute | solution.py:16
  30.4 0.1 constant_dynamic-update-slice_fusion.4
  30.5 9.0 %collective-permute-done.1 = bf16[128,2048]{0,1:T(8,128)(2,1)S(1)} collective-permute-done((bf16[128,2048]{0,1:T(8,128)(2,1)S(1)}, bf16[128,2048]{0,1:T(8,128)(2,1)S(1)}, u32[]{:S(2)}, u32[]{:S(2)}) %collective-permute-start.1) | collective-permute-done | bytes 524320 | tf_op jit(solution)/shard_map/ppermute | solution.py:16
  39.5 0.1 constant_dynamic-update-slice_fusion.3
  39.6 10.8 %collective-permute-done.2 = bf16[128,2048]{0,1:T(8,128)(2,1)S(1)} collective-permute-done((bf16[128,2048]{0,1:T(8,128)(2,1)S(1)}, bf16[128,2048]{0,1:T(8,128)(2,1)S(1)}, u32[]{:S(2)}, u32[]{:S(2)}) %collective-permute-start.2) | collective-permute-done | bytes 524320 | tf_op jit(solution)/shard_map/ppermute | solution.py:16
  50.5 0.1 constant_dynamic-update-slice_fusion.2
  50.6 5.5 %collective-permute-done.3 = bf16[128,2048]{0,1:T(8,128)(2,1)S(1)} collective-permute-done((bf16[128,2048]{0,1:T(8,128)(2,1)S(1)}, bf16[128,2048]{0,1:T(8,128)(2,1)S(1)}, u32[]{:S(2)}, u32[]{:S(2)}) %collective-permute-start.3) | collective-permute-done | bytes 524320 | tf_op jit(solution)/shard_map/ppermute | solution.py:16
  56.1 0.1 constant_dynamic-update-slice_fusion.1
  56.2 0.1 constant_dynamic-update-slice_fusion
  56.3 0.0 copy-start.1
  56.4 1.5 copy-done.1
  57.8 5.9 %fusion.2 = (f32[8,8,128]{2,1,0:T(8,128)S(1)}, f32[8,640,128,8]{2,1,3,0:T(8,128)S(1)}) fusion(pred[128,640]{0,1:T(8,128)(4,1)S(1)} %fusion.11, bf16[128,8,8,128]{3,2,1,0:T(8,128)(2,1)S(1)} %bitcast.69, bf16[640,8,2,128]{0,3,2,1:T(8,128)(2,1)} %bitcast.71), kind=kOutput, calls=%fused_computation.5 | convolution fusion | flops 1357897728 | bytes 24494080 | tf_op jit(solution)/shard_map/rhgd,khd->hgrk/dot_general | solution.py:21
  63.8 5.7 %fusion = f32[8,8,128]{2,1,0:T(8,128)} fusion(f32[8,640,128,8]{2,1,3,0:T(8,128)S(1)} %get-tuple-element.6, f32[8,8,128]{2,1,0:T(8,128)S(1)} %get-tuple-element.5, pred[128,640]{0,1:T(8,128)(4,1)S(1)} %fusion.11), kind=kLoop, calls=%fused_computation.3 | loop fusion | flops 20963328 | bytes 21118976 | tf_op jit(solution)/shard_map/reduce_sum | solution.py:25
  69.5 7.8 %fusion.6 = bf16[128,8,8,128]{0,3,2,1:T(8,128)(2,1)} fusion(f32[8,640,128,8]{2,1,3,0:T(8,128)S(1)} %get-tuple-element.6, f32[8,8,128]{2,1,0:T(8,128)S(1)} %get-tuple-element.5, pred[128,640]{0,1:T(8,128)(4,1)} %copy-done.2, f32[128,8,8]{0,2,1:T(8,128)} %bitcast.76, bf16[640,8,2,128]{0,3,2,1:T(8,128)(2,1)} %bitcast.72), kind=kOutput, calls=%fused_computation.10 | convolution fusion | flops 1365245952 | bytes 24526848 | tf_op jit(solution)/shard_map/hgrk,khd->rhgd/dot_general | solution.py:27
  77.2 6.8 %all-to-all-start = ((bf16[128,16,512]{0,2,1:T(8,128)(2,1)}), bf16[128,16,512]{0,2,1:T(8,128)(2,1)S(1)}, u32[]{:S(2)}, u32[]{:S(2)}) async-start(bf16[128,16,512]{0,2,1:T(8,128)(2,1)} %bitcast.74), calls=%async_computation | async-start | bytes 4194304 | tf_op jit(solution)/shard_map/all_to_all | solution.py:75
  84.1 56.9 %all-gather = s32[16,1,2]{2,1,0:T(1,128)S(1)} all-gather(s32[1,1,2]{2,1,0:T(1,128)S(1)} %bitcast.77), channel_id=1, replica_groups=mesh['groups'=2,'seq'=16] {'seq'}, dimensions={0}, use_global_device_ids=true | all-gather | bytes 136 | tf_op jit(solution)/shard_map/all_gather | solution.py:73
  140.9 0.1 copy.50
  141.0 0.1 compare_select_fusion
  141.1 0.1 reshape.137
  141.3 0.1 copy.68
  141.4 0.0 all-to-all-done
  141.4 0.0 copy-start
  141.4 1.3 copy-done
  142.7 2.9 %copy.61 = bf16[16,128,1,512]{3,1,0,2:T(8,128)(2,1)S(1)} copy(bf16[16,128,1,512]{1,3,0,2:T(8,128)(2,1)} %bitcast.70) | data formatting | bytes 4194304 | tf_op jit(solution)/shard_map/all_to_all | solution.py:75
  145.5 17.3 %gather_fusion = bf16[4096,512]{1,0:T(8,128)(2,1)} fusion(bf16[2048,512]{1,0:T(8,128)(2,1)S(1)} %bitcast.67, s32[4096]{0:T(1024)S(1)} %broadcast_clamp_fusion), kind=kCustom, calls=%fused_computation | custom fusion | bytes 8404992 | tf_op jit(solution)/shard_map/jit(_take)/gather | solution.py:38
  162.9 7.5 %copy_select_fusion = bf16[256,16,512]{2,0,1:T(8,128)(2,1)} fusion(bf16[256,16,512]{2,1,0:T(8,128)(2,1)} %bitcast.68, pred[256,16]{0,1:T(8,128)(4,1)S(1)} %compare_and_fusion), kind=kLoop, calls=%fused_computation.11 | loop fusion | flops 2097152 | bytes 8392704 | tf_op jit(solution)/shard_map/jit(_take)/select_n | solution.py:38
  170.4 4.9 %all-to-all-start.1 = ((bf16[256,16,512]{2,0,1:T(8,128)(2,1)}), bf16[256,16,512]{2,0,1:T(8,128)(2,1)}, u32[]{:S(2)}, u32[]{:S(2)}) async-start(bf16[256,16,512]{2,0,1:T(8,128)(2,1)} %copy_select_fusion), calls=%async_computation.1 | async-start | bytes 8388608 | tf_op jit(solution)/shard_map/all_to_all | solution.py:39
  176.0 0.1 broadcast_bitcast_fusion
  176.0 92.0 %all-to-all-done.1 = bf16[256,16,512]{2,0,1:T(8,128)(2,1)} async-done(((bf16[256,16,512]{2,0,1:T(8,128)(2,1)}), bf16[256,16,512]{2,0,1:T(8,128)(2,1)}, u32[]{:S(2)}, u32[]{:S(2)}) %all-to-all-start.1) | async-done | bytes 4194336 | tf_op jit(solution)/shard_map/all_to_all | solution.py:39
  268.0 6.4 %copy.63 = bf16[256,16,512]{0,2,1:T(8,128)(2,1)} copy(bf16[256,16,512]{2,0,1:T(8,128)(2,1)} %all-to-all-done.1) | data formatting | bytes 8388608 | tf_op jit(solution)/shard_map/all_to_all | solution.py:39
  274.4 4.4 %bitcast_select_fusion.1 = bf16[256,8192]{0,1:T(8,128)(2,1)} fusion(bf16[256,16,512]{0,2,1:T(8,128)(2,1)} %copy.63, pred[256]{0:T(512)(128)(4,1)S(1)} %broadcast_bitcast_fusion), kind=kLoop, calls=%fused_computation.8 | loop fusion | flops 2097152 | bytes 8388864 | tf_op jit(solution)/shard_map/jit(_where)/select_n | solution.py:80
  278.8 6.3 %copy.64 = bf16[256,8192]{1,0:T(8,128)(2,1)} copy(bf16[256,8192]{0,1:T(8,128)(2,1)} %bitcast_select_fusion.1) | data formatting | bytes 8388608 | tf_op jit(solution)/shard_map/jit(_where)/select_n | solution.py:80
  (19 shorter events, 0.1 us)
Async XLA Ops:
  0.0 24.9 %copy-start.4 = (s32[128]{0:T(128)S(1)}, s32[128]{0:T(128)}, u32[]{:S(2)}) copy-start(s32[128]{0:T(128)} %param.7) | copy-start | bytes 1540
  0.7 18.0 %collective-permute-start.4 = (s32[128]{0:T(128)S(1)}, s32[128]{0:T(128)S(1)}, u32[]{:S(2)}, u32[]{:S(2)}) collective-permute-start(s32[128]{0:T(128)S(1)} %broadcast_add_fusion), channel_id=1, source_target_pairs={{0,4},{1,5},{2,6},{3,7},{4,8},{5,9},{6,10},{7,11},{8,12},{9,13},{1... | collective-permute-start | bytes 1544 | tf_op jit(solution)/shard_map/ppermute | solution.py:16
  3.9 16.8 %collective-permute-start.5 = (s32[128]{0:T(128)S(1)}, s32[128]{0:T(128)S(1)}, u32[]{:S(2)}, u32[]{:S(2)}) collective-permute-start(s32[128]{0:T(128)S(1)} %broadcast_add_fusion), channel_id=1, source_target_pairs={{0,3},{1,4},{2,5},{3,6},{4,7},{5,8},{6,9},{7,10},{8,11},{9,12},{10... | collective-permute-start | bytes 1544 | tf_op jit(solution)/shard_map/ppermute | solution.py:16
  8.0 14.7 %collective-permute-start.6 = (s32[128]{0:T(128)S(1)}, s32[128]{0:T(128)S(1)}, u32[]{:S(2)}, u32[]{:S(2)}) collective-permute-start(s32[128]{0:T(128)S(1)} %broadcast_add_fusion), channel_id=1, source_target_pairs={{0,2},{1,3},{2,4},{3,5},{4,6},{5,7},{6,8},{7,9},{8,10},{9,11},{10,... | collective-permute-start | bytes 1544 | tf_op jit(solution)/shard_map/ppermute | solution.py:16
  9.9 15.0 %collective-permute-start.7 = (s32[128]{0:T(128)S(1)}, s32[128]{0:T(128)S(1)}, u32[]{:S(2)}, u32[]{:S(2)}) collective-permute-start(s32[128]{0:T(128)S(1)} %broadcast_add_fusion), channel_id=1, source_target_pairs={{0,1},{1,2},{2,3},{3,4},{4,5},{5,6},{6,7},{7,8},{8,9},{9,10},{10,1... | collective-permute-start | bytes 1544 | tf_op jit(solution)/shard_map/ppermute | solution.py:16
  14.6 15.8 %collective-permute-start = (bf16[128,2048]{0,1:T(8,128)(2,1)S(1)}, bf16[128,2048]{0,1:T(8,128)(2,1)S(1)}, u32[]{:S(2)}, u32[]{:S(2)}) collective-permute-start(bf16[128,2048]{0,1:T(8,128)(2,1)S(1)} %copy.52), channel_id=1, source_target_pairs={{0,4},{1,5},{2,6},{3,7},{4,8},{5,9},{6,10},{7,11},{8,12},{9,13},{1... | collective-permute-start | bytes 1572872 | tf_op jit(solution)/shard_map/ppermute | solution.py:16
  18.8 20.7 %collective-permute-start.1 = (bf16[128,2048]{0,1:T(8,128)(2,1)S(1)}, bf16[128,2048]{0,1:T(8,128)(2,1)S(1)}, u32[]{:S(2)}, u32[]{:S(2)}) collective-permute-start(bf16[128,2048]{0,1:T(8,128)(2,1)S(1)} %copy.52), channel_id=1, source_target_pairs={{0,3},{1,4},{2,5},{3,6},{4,7},{5,8},{6,9},{7,10},{8,11},{9,12},{10... | collective-permute-start | bytes 1572872 | tf_op jit(solution)/shard_map/ppermute | solution.py:16
  20.7 29.8 %collective-permute-start.2 = (bf16[128,2048]{0,1:T(8,128)(2,1)S(1)}, bf16[128,2048]{0,1:T(8,128)(2,1)S(1)}, u32[]{:S(2)}, u32[]{:S(2)}) collective-permute-start(bf16[128,2048]{0,1:T(8,128)(2,1)S(1)} %copy.52), channel_id=1, source_target_pairs={{0,2},{1,3},{2,4},{3,5},{4,6},{5,7},{6,8},{7,9},{8,10},{9,11},{10,... | collective-permute-start | bytes 1572872 | tf_op jit(solution)/shard_map/ppermute | solution.py:16
  22.7 33.4 %collective-permute-start.3 = (bf16[128,2048]{0,1:T(8,128)(2,1)S(1)}, bf16[128,2048]{0,1:T(8,128)(2,1)S(1)}, u32[]{:S(2)}, u32[]{:S(2)}) collective-permute-start(bf16[128,2048]{0,1:T(8,128)(2,1)S(1)} %copy.52), channel_id=1, source_target_pairs={{0,1},{1,2},{2,3},{3,4},{4,5},{5,6},{6,7},{7,8},{8,9},{9,10},{10,1... | collective-permute-start | bytes 1572872 | tf_op jit(solution)/shard_map/ppermute | solution.py:16
  25.1 38.7 %copy-start.2 = (pred[128,640]{0,1:T(8,128)(4,1)}, pred[128,640]{0,1:T(8,128)(4,1)S(1)}, u32[]{:S(2)}) copy-start(pred[128,640]{0,1:T(8,128)(4,1)S(1)} %fusion.11) | copy-start | bytes 245764
  56.3 1.5 copy-start.1
  77.2 6.8 %copy-start.3 = (s32[1,2]{1,0:T(1,128)S(1)}, s32[1,2]{1,0:T(1,128)}, u32[]{:S(2)}) copy-start(s32[1,2]{1,0:T(1,128)} %param.8) | copy-start | bytes 28
  77.2 64.1 %all-to-all-start = ((bf16[128,16,512]{0,2,1:T(8,128)(2,1)}), bf16[128,16,512]{0,2,1:T(8,128)(2,1)S(1)}, u32[]{:S(2)}, u32[]{:S(2)}) async-start(bf16[128,16,512]{0,2,1:T(8,128)(2,1)} %bitcast.74), calls=%async_computation | async-start | bytes 4194304 | tf_op jit(solution)/shard_map/all_to_all | solution.py:75
  141.4 1.3 copy-start
  170.4 97.6 %all-to-all-start.1 = ((bf16[256,16,512]{2,0,1:T(8,128)(2,1)}), bf16[256,16,512]{2,0,1:T(8,128)(2,1)}, u32[]{:S(2)}, u32[]{:S(2)}) async-start(bf16[256,16,512]{2,0,1:T(8,128)(2,1)} %copy_select_fusion), calls=%async_computation.1 | async-start | bytes 8388608 | tf_op jit(solution)/shard_map/all_to_all | solution.py:39
where the time goes:
time: 286 us; the launch traced here: 285 us
  waiting for transfers between devices  123 us (43%)
  blocking collectives  56.9 us (20%)
  local copies, waits for them, and re-layouts  40.1 us (14%)
  starting transfers between devices  32.2 us (11%)
  other arithmetic  18.6 us (7%)
  matrix products  13.7 us (5%)
    all_to_all x1, waiting for transfers between devices, deliver_owners(): lax.all_to_all(send_rows, 'seq', split_axis=1, concat_axis=1, tiled=True)  92 us
    all_gather x1, blocking collectives, local(): all_lists = lax.all_gather(owner_tiles, 'seq', axis=0, tiled=True)  56.9 us
    ppermute x8, waiting for transfers between devices, from_behind(): return lax.ppermute(shard, axis, pairs)  30.7 us
    ppermute x8, starting transfers between devices, from_behind(): return lax.ppermute(shard, axis, pairs)  20.5 us
    gather x1, local copies, waits for them, and re-layouts, deliver_owners(): jnp.take(head_rows, row_index.reshape(slot_rows, seq_count), axis=0)  17.3 us
    dot_general x1, matrix products, attend(): jnp.einsum('hgrk,khd->rhgd', weights, value_rows, preferred_element_type=...  7.78 us
    select_n x2, other arithmetic, deliver_owners(): jnp.take(head_rows, row_index.reshape(slot_rows, seq_count), axis=0)  7.62 us
    all_to_all x1, starting transfers between devices, local(): lax.all_to_all(out_send, 'seq', split_axis=1, concat_axis=0, tiled=True)  6.8 us
  transfers between devices with their start and end apart: 10, of which 5 were waited for; matrix products, arithmetic and copies ran while one was open for 2% of the time, Pallas kernels for 0%

commit v1 on v0

--- a/solution.py
+++ b/solution.py
@@ -70,7 +70,12 @@
         allowed,
     )
     local_out = local_out.reshape(token_per_holder, width)
-    all_lists = lax.all_gather(owner_tiles, "seq", axis=0, tiled=True)
+    ring = [owner_tiles]
+    for hop in range(15):
+        ring.append(lax.ppermute(ring[-1], "seq", [(dev, (dev + 1) % 16) for dev in range(16)]))
+    all_lists = jnp.roll(
+        jnp.concatenate(ring[::-1], axis=0), (lax.axis_index("seq") + 1) * ring[0].shape[0], axis=0
+    )
     out_send = local_out.reshape(token_per_holder, seq_count, head_cols)
     head_rows = lax.all_to_all(out_send, "seq", split_axis=1, concat_axis=0, tiled=True).reshape(
         token_per_holder * seq_count, head_cols

time: 286 us -> 348 us (1.22)
  starting transfers between devices: 32.2 us -> 96.8 us
  blocking collectives: 56.9 us -> 0 us
  waiting for transfers between devices: 123 us -> 176 us
    all_gather x1 -> x0, blocking collectives: 56.9 us -> none  [local(): all_lists = lax.all_gather(owner_tiles, 'seq', axis=0, tiled=True)]
    ppermute x0 -> x15, waiting for transfers between devices: none -> 53.8 us  [local(): lax.ppermute(ring[-1], 'seq', [(dev, (dev + 1) % 16) for dev in range(16)])]
    ppermute x0 -> x15, starting transfers between devices: none -> 46 us  [local(): lax.ppermute(ring[-1], 'seq', [(dev, (dev + 1) % 16) for dev in range(16)])]
    all_to_all x1, starting transfers between devices: 4.89 us -> 23.5 us  [deliver_owners(): lax.all_to_all(send_rows, 'seq', split_axis=1, concat_axis=1, tiled=True)]
  transfers between devices with their start and end apart: 10 -> 25, of which waited for: 5 -> 20; matrix products, arithmetic and copies ran while one was open for 2% -> 1% of each run, Pallas kernels for 0% -> 0%
where the time goes in v1:
time: 348 us; the launch traced here: 347 us
  waiting for transfers between devices  176 us (51%)
  starting transfers between devices  96.8 us (28%)
  local copies, waits for them, and re-layouts  40.3 us (12%)
  other arithmetic  18.8 us (5%)
  matrix products  13.7 us (4%)
    all_to_all x1, waiting for transfers between devices, deliver_owners(): lax.all_to_all(send_rows, 'seq', split_axis=1, concat_axis=1, tiled=True)  91.7 us
    ppermute x15, waiting for transfers between devices, local(): lax.ppermute(ring[-1], 'seq', [(dev, (dev + 1) % 16) for dev in range(16)])  53.8 us
    ppermute x15, starting transfers between devices, local(): lax.ppermute(ring[-1], 'seq', [(dev, (dev + 1) % 16) for dev in range(16)])  46 us
    ppermute x8, waiting for transfers between devices, from_behind(): return lax.ppermute(shard, axis, pairs)  30.7 us
    all_to_all x1, starting transfers between devices, deliver_owners(): lax.all_to_all(send_rows, 'seq', split_axis=1, concat_axis=1, tiled=True)  23.5 us
    ppermute x8, starting transfers between devices, from_behind(): return lax.ppermute(shard, axis, pairs)  20.5 us
    gather x1, local copies, waits for them, and re-layouts, deliver_owners(): jnp.take(head_rows, row_index.reshape(slot_rows, seq_count), axis=0)  17.3 us
    dot_general x1, matrix products, attend(): jnp.einsum('hgrk,khd->rhgd', weights, value_rows, preferred_element_type=...  7.79 us
  transfers between devices with their start and end apart: 25, of which 20 were waited for; matrix products, arithmetic and copies ran while one was open for 1% of the time, Pallas kernels for 0%

profile of v1, /device:TPU:15, one launch (start us, length us, event | category | flops | bytes accessed | tf_op | source)
XLA Modules:
  0.0 346.8 jit_solution(13325079592044438856)
XLA Ops:
  0.0 0.7 broadcast_add_fusion
  0.7 3.2 collective-permute-start.19
  3.9 4.0 %collective-permute-start.20 = (s32[128]{0:T(128)S(1)}, s32[128]{0:T(128)S(1)}, u32[]{:S(2)}, u32[]{:S(2)}) collective-permute-start(s32[128]{0:T(128)S(1)} %broadcast_add_fusion), channel_id=1, source_target_pairs={{0,3},{1,4},{2,5},{3,6},{4,7},{5,8},{6,9},{7,10},{8,11},{9,12},{10... | collective-permute-start | bytes 1544 | tf_op jit(solution)/shard_map/ppermute | solution.py:16
  8.0 1.9 collective-permute-start.21
  9.9 3.4 collective-permute-start.22
  13.3 1.3 copy.41
  14.6 1.9 collective-permute-start.15
  16.6 2.2 copy.60
  18.8 1.9 collective-permute-start.16
  20.7 1.9 collective-permute-start.17
  22.7 2.2 collective-permute-start.18
  25.1 5.3 %collective-permute-done.15 = bf16[128,2048]{0,1:T(8,128)(2,1)S(1)} collective-permute-done((bf16[128,2048]{0,1:T(8,128)(2,1)S(1)}, bf16[128,2048]{0,1:T(8,128)(2,1)S(1)}, u32[]{:S(2)}, u32[]{:S(2)}) %collective-permute-start.15) | collective-permute-done | bytes 524320 | tf_op jit(solution)/shard_map/ppermute | solution.py:16
  30.5 9.0 %collective-permute-done.16 = bf16[128,2048]{0,1:T(8,128)(2,1)S(1)} collective-permute-done((bf16[128,2048]{0,1:T(8,128)(2,1)S(1)}, bf16[128,2048]{0,1:T(8,128)(2,1)S(1)}, u32[]{:S(2)}, u32[]{:S(2)}) %collective-permute-start.16) | collective-permute-done | bytes 524320 | tf_op jit(solution)/shard_map/ppermute | solution.py:16
  39.6 10.8 %collective-permute-done.17 = bf16[128,2048]{0,1:T(8,128)(2,1)S(1)} collective-permute-done((bf16[128,2048]{0,1:T(8,128)(2,1)S(1)}, bf16[128,2048]{0,1:T(8,128)(2,1)S(1)}, u32[]{:S(2)}, u32[]{:S(2)}) %collective-permute-start.17) | collective-permute-done | bytes 524320 | tf_op jit(solution)/shard_map/ppermute | solution.py:16
  50.6 5.5 %collective-permute-done.18 = bf16[128,2048]{0,1:T(8,128)(2,1)S(1)} collective-permute-done((bf16[128,2048]{0,1:T(8,128)(2,1)S(1)}, bf16[128,2048]{0,1:T(8,128)(2,1)S(1)}, u32[]{:S(2)}, u32[]{:S(2)}) %collective-permute-start.18) | collective-permute-done | bytes 524320 | tf_op jit(solution)/shard_map/ppermute | solution.py:16
  56.4 1.5 copy-done.1
  57.8 5.9 %fusion.2 = (f32[8,8,128]{2,1,0:T(8,128)S(1)}, f32[8,640,128,8]{2,1,3,0:T(8,128)S(1)}) fusion(pred[128,640]{0,1:T(8,128)(4,1)S(1)} %fusion.11, bf16[128,8,8,128]{3,2,1,0:T(8,128)(2,1)S(1)} %bitcast.66, bf16[640,8,2,128]{0,3,2,1:T(8,128)(2,1)} %bitcast.68), kind=kOutput, calls=%fused_computation.5 | convolution fusion | flops 1357897728 | bytes 24494080 | tf_op jit(solution)/shard_map/rhgd,khd->hgrk/dot_general | solution.py:21
  63.8 5.7 %fusion = f32[8,8,128]{2,1,0:T(8,128)} fusion(f32[8,640,128,8]{2,1,3,0:T(8,128)S(1)} %get-tuple-element.6, f32[8,8,128]{2,1,0:T(8,128)S(1)} %get-tuple-element.5, pred[128,640]{0,1:T(8,128)(4,1)S(1)} %fusion.11), kind=kLoop, calls=%fused_computation.3 | loop fusion | flops 20963328 | bytes 21118976 | tf_op jit(solution)/shard_map/reduce_sum | solution.py:25
  69.5 7.8 %fusion.6 = bf16[128,8,8,128]{0,3,2,1:T(8,128)(2,1)} fusion(f32[8,640,128,8]{2,1,3,0:T(8,128)S(1)} %get-tuple-element.6, f32[8,8,128]{2,1,0:T(8,128)S(1)} %get-tuple-element.5, pred[128,640]{0,1:T(8,128)(4,1)} %copy-done.2, f32[128,8,8]{0,2,1:T(8,128)} %bitcast.73, bf16[640,8,2,128]{0,3,2,1:T(8,128)(2,1)} %bitcast.69), kind=kOutput, calls=%fused_computation.10 | convolution fusion | flops 1365245952 | bytes 24526848 | tf_op jit(solution)/shard_map/hgrk,khd->rhgd/dot_general | solution.py:27
  77.3 6.8 %all-to-all-start = ((bf16[128,16,512]{0,2,1:T(8,128)(2,1)}), bf16[128,16,512]{0,2,1:T(8,128)(2,1)S(1)}, u32[]{:S(2)}, u32[]{:S(2)}) async-start(bf16[128,16,512]{0,2,1:T(8,128)(2,1)} %bitcast.71), calls=%async_computation | async-start | bytes 4194304 | tf_op jit(solution)/shard_map/all_to_all | solution.py:80
  84.2 1.5 collective-permute-start
  85.6 43.7 %collective-permute-done = s32[1,2]{0,1:T(2,128)S(1)} collective-permute-done((s32[1,2]{0,1:T(2,128)S(1)}, s32[1,2]{0,1:T(2,128)S(1)}, u32[]{:S(2)}, u32[]{:S(2)}) %collective-permute-start) | collective-permute-done | bytes 40 | tf_op jit(solution)/shard_map/ppermute | solution.py:75
  129.3 3.3 collective-permute-start.1
  133.3 3.2 collective-permute-start.2
  137.2 3.2 collective-permute-start.3
  140.4 0.7 collective-permute-done.3
  141.1 3.2 collective-permute-start.4
  145.0 3.2 collective-permute-start.5
  148.9 3.2 collective-permute-start.6
  152.1 0.7 collective-permute-done.6
  152.8 3.2 collective-permute-start.7
  156.7 3.2 collective-permute-start.8
  159.9 0.7 collective-permute-done.8
  160.6 3.2 collective-permute-start.9
  164.5 3.2 collective-permute-start.10
  168.4 3.2 collective-permute-start.11
  172.3 3.2 collective-permute-start.12
  176.2 3.2 collective-permute-start.13
  180.1 3.2 collective-permute-start.14
  184.6 1.3 copy-done
  185.9 2.9 copy.50
  188.7 17.3 %gather_fusion = bf16[4096,512]{1,0:T(8,128)(2,1)} fusion(bf16[2048,512]{1,0:T(8,128)(2,1)S(1)} %bitcast.64, s32[4096]{0:T(1024)S(1)} %broadcast_clamp_fusion), kind=kCustom, calls=%fused_computation | custom fusion | bytes 8404992 | tf_op jit(solution)/shard_map/jit(_take)/gather | solution.py:38
  206.1 7.6 %copy_select_fusion = bf16[256,16,512]{2,0,1:T(8,128)(2,1)} fusion(bf16[256,16,512]{2,1,0:T(8,128)(2,1)} %bitcast.65, pred[256,16]{0,1:T(8,128)(4,1)S(1)} %compare_and_fusion), kind=kLoop, calls=%fused_computation.11 | loop fusion | flops 2097152 | bytes 8392704 | tf_op jit(solution)/shard_map/jit(_take)/select_n | solution.py:38
  213.6 23.5 %all-to-all-start.1 = ((bf16[256,16,512]{2,0,1:T(8,128)(2,1)}), bf16[256,16,512]{2,0,1:T(8,128)(2,1)}, u32[]{:S(2)}, u32[]{:S(2)}) async-start(bf16[256,16,512]{2,0,1:T(8,128)(2,1)} %copy_select_fusion), calls=%async_computation.1 | async-start | bytes 8388608 | tf_op jit(solution)/shard_map/all_to_all | solution.py:39
  237.9 91.7 %all-to-all-done.1 = bf16[256,16,512]{2,0,1:T(8,128)(2,1)} async-done(((bf16[256,16,512]{2,0,1:T(8,128)(2,1)}), bf16[256,16,512]{2,0,1:T(8,128)(2,1)}, u32[]{:S(2)}, u32[]{:S(2)}) %all-to-all-start.1) | async-done | bytes 4194336 | tf_op jit(solution)/shard_map/all_to_all | solution.py:39
  329.6 6.4 %copy.52 = bf16[256,16,512]{0,2,1:T(8,128)(2,1)} copy(bf16[256,16,512]{2,0,1:T(8,128)(2,1)} %all-to-all-done.1) | data formatting | bytes 8388608 | tf_op jit(solution)/shard_map/all_to_all | solution.py:39
  336.0 4.4 %bitcast_select_fusion.1 = bf16[256,8192]{0,1:T(8,128)(2,1)} fusion(bf16[256,16,512]{0,2,1:T(8,128)(2,1)} %copy.52, pred[256]{0:T(512)(128)(4,1)S(1)} %broadcast_bitcast_fusion), kind=kLoop, calls=%fused_computation.8 | loop fusion | flops 2097152 | bytes 8388864 | tf_op jit(solution)/shard_map/jit(_where)/select_n | solution.py:85
  340.4 6.3 %copy.53 = bf16[256,8192]{1,0:T(8,128)(2,1)} copy(bf16[256,8192]{0,1:T(8,128)(2,1)} %bitcast_select_fusion.1) | data formatting | bytes 8388608 | tf_op jit(solution)/shard_map/jit(_where)/select_n | solution.py:85
  (49 shorter events, 9.5 us)
Async XLA Ops:
  0.0 24.9 %copy-start.3 = (s32[128]{0:T(128)S(1)}, s32[128]{0:T(128)}, u32[]{:S(2)}) copy-start(s32[128]{0:T(128)} %param.7) | copy-start | bytes 1540
  0.7 18.0 %collective-permute-start.19 = (s32[128]{0:T(128)S(1)}, s32[128]{0:T(128)S(1)}, u32[]{:S(2)}, u32[]{:S(2)}) collective-permute-start(s32[128]{0:T(128)S(1)} %broadcast_add_fusion), channel_id=1, source_target_pairs={{0,4},{1,5},{2,6},{3,7},{4,8},{5,9},{6,10},{7,11},{8,12},{9,13},{1... | collective-permute-start | bytes 1544 | tf_op jit(solution)/shard_map/ppermute | solution.py:16
  3.9 16.8 %collective-permute-start.20 = (s32[128]{0:T(128)S(1)}, s32[128]{0:T(128)S(1)}, u32[]{:S(2)}, u32[]{:S(2)}) collective-permute-start(s32[128]{0:T(128)S(1)} %broadcast_add_fusion), channel_id=1, source_target_pairs={{0,3},{1,4},{2,5},{3,6},{4,7},{5,8},{6,9},{7,10},{8,11},{9,12},{10... | collective-permute-start | bytes 1544 | tf_op jit(solution)/shard_map/ppermute | solution.py:16
  8.0 14.7 %collective-permute-start.21 = (s32[128]{0:T(128)S(1)}, s32[128]{0:T(128)S(1)}, u32[]{:S(2)}, u32[]{:S(2)}) collective-permute-start(s32[128]{0:T(128)S(1)} %broadcast_add_fusion), channel_id=1, source_target_pairs={{0,2},{1,3},{2,4},{3,5},{4,6},{5,7},{6,8},{7,9},{8,10},{9,11},{10,... | collective-permute-start | bytes 1544 | tf_op jit(solution)/shard_map/ppermute | solution.py:16
  9.9 15.0 %collective-permute-start.22 = (s32[128]{0:T(128)S(1)}, s32[128]{0:T(128)S(1)}, u32[]{:S(2)}, u32[]{:S(2)}) collective-permute-start(s32[128]{0:T(128)S(1)} %broadcast_add_fusion), channel_id=1, source_target_pairs={{0,1},{1,2},{2,3},{3,4},{4,5},{5,6},{6,7},{7,8},{8,9},{9,10},{10,1... | collective-permute-start | bytes 1544 | tf_op jit(solution)/shard_map/ppermute | solution.py:16
  14.6 15.8 %collective-permute-start.15 = (bf16[128,2048]{0,1:T(8,128)(2,1)S(1)}, bf16[128,2048]{0,1:T(8,128)(2,1)S(1)}, u32[]{:S(2)}, u32[]{:S(2)}) collective-permute-start(bf16[128,2048]{0,1:T(8,128)(2,1)S(1)} %copy.41), channel_id=1, source_target_pairs={{0,4},{1,5},{2,6},{3,7},{4,8},{5,9},{6,10},{7,11},{8,12},{9,13},{1... | collective-permute-start | bytes 1572872 | tf_op jit(solution)/shard_map/ppermute | solution.py:16
  18.8 20.7 %collective-permute-start.16 = (bf16[128,2048]{0,1:T(8,128)(2,1)S(1)}, bf16[128,2048]{0,1:T(8,128)(2,1)S(1)}, u32[]{:S(2)}, u32[]{:S(2)}) collective-permute-start(bf16[128,2048]{0,1:T(8,128)(2,1)S(1)} %copy.41), channel_id=1, source_target_pairs={{0,3},{1,4},{2,5},{3,6},{4,7},{5,8},{6,9},{7,10},{8,11},{9,12},{10... | collective-permute-start | bytes 1572872 | tf_op jit(solution)/shard_map/ppermute | solution.py:16
  20.7 29.8 %collective-permute-start.17 = (bf16[128,2048]{0,1:T(8,128)(2,1)S(1)}, bf16[128,2048]{0,1:T(8,128)(2,1)S(1)}, u32[]{:S(2)}, u32[]{:S(2)}) collective-permute-start(bf16[128,2048]{0,1:T(8,128)(2,1)S(1)} %copy.41), channel_id=1, source_target_pairs={{0,2},{1,3},{2,4},{3,5},{4,6},{5,7},{6,8},{7,9},{8,10},{9,11},{10,... | collective-permute-start | bytes 1572872 | tf_op jit(solution)/shard_map/ppermute | solution.py:16
  22.7 33.4 %collective-permute-start.18 = (bf16[128,2048]{0,1:T(8,128)(2,1)S(1)}, bf16[128,2048]{0,1:T(8,128)(2,1)S(1)}, u32[]{:S(2)}, u32[]{:S(2)}) collective-permute-start(bf16[128,2048]{0,1:T(8,128)(2,1)S(1)} %copy.41), channel_id=1, source_target_pairs={{0,1},{1,2},{2,3},{3,4},{4,5},{5,6},{6,7},{7,8},{8,9},{9,10},{10,1... | collective-permute-start | bytes 1572872 | tf_op jit(solution)/shard_map/ppermute | solution.py:16
  25.1 38.7 %copy-start.2 = (pred[128,640]{0,1:T(8,128)(4,1)}, pred[128,640]{0,1:T(8,128)(4,1)S(1)}, u32[]{:S(2)}) copy-start(pred[128,640]{0,1:T(8,128)(4,1)S(1)} %fusion.11) | copy-start | bytes 245764
  56.3 1.5 copy-start.1
  77.3 6.8 %copy-start.4 = (s32[1,2]{1,0:T(1,128)S(1)}, s32[1,2]{1,0:T(1,128)}, u32[]{:S(2)}) copy-start(s32[1,2]{1,0:T(1,128)} %param.8) | copy-start | bytes 28
  77.3 107.3 %all-to-all-start = ((bf16[128,16,512]{0,2,1:T(8,128)(2,1)}), bf16[128,16,512]{0,2,1:T(8,128)(2,1)S(1)}, u32[]{:S(2)}, u32[]{:S(2)}) async-start(bf16[128,16,512]{0,2,1:T(8,128)(2,1)} %bitcast.71), calls=%async_computation | async-start | bytes 4194304 | tf_op jit(solution)/shard_map/all_to_all | solution.py:80
  84.2 45.1 %collective-permute-start = (s32[1,2]{0,1:T(2,128)S(1)}, s32[1,2]{0,1:T(2,128)S(1)}, u32[]{:S(2)}, u32[]{:S(2)}) collective-permute-start(s32[1,2]{0,1:T(2,128)S(1)} %copy.37), channel_id=1, source_target_pairs={{0,1},{1,2},{2,3},{3,4},{4,5},{5,6},{6,7},{7,8},{8,9},{9,10},{10,1... | collective-permute-start | bytes 32 | tf_op jit(solution)/shard_map/ppermute | solution.py:75
  129.3 4.0 %collective-permute-start.1 = (s32[1,2]{0,1:T(2,128)S(1)}, s32[1,2]{0,1:T(2,128)S(1)}, u32[]{:S(2)}, u32[]{:S(2)}) collective-permute-start(s32[1,2]{0,1:T(2,128)S(1)} %collective-permute-done), channel_id=1, source_target_pairs={{0,1},{1,2},{2,3},{3,4},{4,5},{5,6},{6,7},{7,8},{8,9},{9,10},{10,1... | collective-permute-start | bytes 32 | tf_op jit(solution)/shard_map/ppermute | solution.py:75
  133.3 3.9 %collective-permute-start.2 = (s32[1,2]{0,1:T(2,128)S(1)}, s32[1,2]{0,1:T(2,128)S(1)}, u32[]{:S(2)}, u32[]{:S(2)}) collective-permute-start(s32[1,2]{0,1:T(2,128)S(1)} %collective-permute-done.1), channel_id=1, source_target_pairs={{0,1},{1,2},{2,3},{3,4},{4,5},{5,6},{6,7},{7,8},{8,9},{9,10},{10,1... | collective-permute-start | bytes 32 | tf_op jit(solution)/shard_map/ppermute | solution.py:75
  137.2 3.9 %collective-permute-start.3 = (s32[1,2]{0,1:T(2,128)S(1)}, s32[1,2]{0,1:T(2,128)S(1)}, u32[]{:S(2)}, u32[]{:S(2)}) collective-permute-start(s32[1,2]{0,1:T(2,128)S(1)} %collective-permute-done.2), channel_id=1, source_target_pairs={{0,1},{1,2},{2,3},{3,4},{4,5},{5,6},{6,7},{7,8},{8,9},{9,10},{10,1... | collective-permute-start | bytes 32 | tf_op jit(solution)/shard_map/ppermute | solution.py:75
  141.1 3.9 %collective-permute-start.4 = (s32[1,2]{0,1:T(2,128)S(1)}, s32[1,2]{0,1:T(2,128)S(1)}, u32[]{:S(2)}, u32[]{:S(2)}) collective-permute-start(s32[1,2]{0,1:T(2,128)S(1)} %collective-permute-done.3), channel_id=1, source_target_pairs={{0,1},{1,2},{2,3},{3,4},{4,5},{5,6},{6,7},{7,8},{8,9},{9,10},{10,1... | collective-permute-start | bytes 32 | tf_op jit(solution)/shard_map/ppermute | solution.py:75
  145.0 3.9 %collective-permute-start.5 = (s32[1,2]{0,1:T(2,128)S(1)}, s32[1,2]{0,1:T(2,128)S(1)}, u32[]{:S(2)}, u32[]{:S(2)}) collective-permute-start(s32[1,2]{0,1:T(2,128)S(1)} %collective-permute-done.4), channel_id=1, source_target_pairs={{0,1},{1,2},{2,3},{3,4},{4,5},{5,6},{6,7},{7,8},{8,9},{9,10},{10,1... | collective-permute-start | bytes 32 | tf_op jit(solution)/shard_map/ppermute | solution.py:75
  148.9 3.9 %collective-permute-start.6 = (s32[1,2]{0,1:T(2,128)S(1)}, s32[1,2]{0,1:T(2,128)S(1)}, u32[]{:S(2)}, u32[]{:S(2)}) collective-permute-start(s32[1,2]{0,1:T(2,128)S(1)} %collective-permute-done.5), channel_id=1, source_target_pairs={{0,1},{1,2},{2,3},{3,4},{4,5},{5,6},{6,7},{7,8},{8,9},{9,10},{10,1... | collective-permute-start | bytes 32 | tf_op jit(solution)/shard_map/ppermute | solution.py:75
  152.8 3.9 %collective-permute-start.7 = (s32[1,2]{0,1:T(2,128)S(1)}, s32[1,2]{0,1:T(2,128)S(1)}, u32[]{:S(2)}, u32[]{:S(2)}) collective-permute-start(s32[1,2]{0,1:T(2,128)S(1)} %collective-permute-done.6), channel_id=1, source_target_pairs={{0,1},{1,2},{2,3},{3,4},{4,5},{5,6},{6,7},{7,8},{8,9},{9,10},{10,1... | collective-permute-start | bytes 32 | tf_op jit(solution)/shard_map/ppermute | solution.py:75
  156.7 3.9 %collective-permute-start.8 = (s32[1,2]{0,1:T(2,128)S(1)}, s32[1,2]{0,1:T(2,128)S(1)}, u32[]{:S(2)}, u32[]{:S(2)}) collective-permute-start(s32[1,2]{0,1:T(2,128)S(1)} %collective-permute-done.7), channel_id=1, source_target_pairs={{0,1},{1,2},{2,3},{3,4},{4,5},{5,6},{6,7},{7,8},{8,9},{9,10},{10,1... | collective-permute-start | bytes 32 | tf_op jit(solution)/shard_map/ppermute | solution.py:75
  160.6 3.9 %collective-permute-start.9 = (s32[1,2]{0,1:T(2,128)S(1)}, s32[1,2]{0,1:T(2,128)S(1)}, u32[]{:S(2)}, u32[]{:S(2)}) collective-permute-start(s32[1,2]{0,1:T(2,128)S(1)} %collective-permute-done.8), channel_id=1, source_target_pairs={{0,1},{1,2},{2,3},{3,4},{4,5},{5,6},{6,7},{7,8},{8,9},{9,10},{10,1... | collective-permute-start | bytes 32 | tf_op jit(solution)/shard_map/ppermute | solution.py:75
  164.5 3.9 %collective-permute-start.10 = (s32[1,2]{0,1:T(2,128)S(1)}, s32[1,2]{0,1:T(2,128)S(1)}, u32[]{:S(2)}, u32[]{:S(2)}) collective-permute-start(s32[1,2]{0,1:T(2,128)S(1)} %collective-permute-done.9), channel_id=1, source_target_pairs={{0,1},{1,2},{2,3},{3,4},{4,5},{5,6},{6,7},{7,8},{8,9},{9,10},{10,1... | collective-permute-start | bytes 32 | tf_op jit(solution)/shard_map/ppermute | solution.py:75
  168.4 3.9 %collective-permute-start.11 = (s32[1,2]{0,1:T(2,128)S(1)}, s32[1,2]{0,1:T(2,128)S(1)}, u32[]{:S(2)}, u32[]{:S(2)}) collective-permute-start(s32[1,2]{0,1:T(2,128)S(1)} %collective-permute-done.10), channel_id=1, source_target_pairs={{0,1},{1,2},{2,3},{3,4},{4,5},{5,6},{6,7},{7,8},{8,9},{9,10},{10,1... | collective-permute-start | bytes 32 | tf_op jit(solution)/shard_map/ppermute | solution.py:75
  172.3 3.9 %collective-permute-start.12 = (s32[1,2]{0,1:T(2,128)S(1)}, s32[1,2]{0,1:T(2,128)S(1)}, u32[]{:S(2)}, u32[]{:S(2)}) collective-permute-start(s32[1,2]{0,1:T(2,128)S(1)} %collective-permute-done.11), channel_id=1, source_target_pairs={{0,1},{1,2},{2,3},{3,4},{4,5},{5,6},{6,7},{7,8},{8,9},{9,10},{10,1... | collective-permute-start | bytes 32 | tf_op jit(solution)/shard_map/ppermute | solution.py:75
  176.2 3.9 %collective-permute-start.13 = (s32[1,2]{0,1:T(2,128)S(1)}, s32[1,2]{0,1:T(2,128)S(1)}, u32[]{:S(2)}, u32[]{:S(2)}) collective-permute-start(s32[1,2]{0,1:T(2,128)S(1)} %collective-permute-done.12), channel_id=1, source_target_pairs={{0,1},{1,2},{2,3},{3,4},{4,5},{5,6},{6,7},{7,8},{8,9},{9,10},{10,1... | collective-permute-start | bytes 32 | tf_op jit(solution)/shard_map/ppermute | solution.py:75
  180.1 3.9 %collective-permute-start.14 = (s32[1,2]{0,1:T(2,128)S(1)}, s32[1,2]{0,1:T(2,128)S(1)}, u32[]{:S(2)}, u32[]{:S(2)}) collective-permute-start(s32[1,2]{0,1:T(2,128)S(1)} %collective-permute-done.13), channel_id=1, source_target_pairs={{0,1},{1,2},{2,3},{3,4},{4,5},{5,6},{6,7},{7,8},{8,9},{9,10},{10,1... | collective-permute-start | bytes 32 | tf_op jit(solution)/shard_map/ppermute | solution.py:75
  184.5 1.3 copy-start
  213.6 116.0 %all-to-all-start.1 = ((bf16[256,16,512]{2,0,1:T(8,128)(2,1)}), bf16[256,16,512]{2,0,1:T(8,128)(2,1)}, u32[]{:S(2)}, u32[]{:S(2)}) async-start(bf16[256,16,512]{2,0,1:T(8,128)(2,1)} %copy_select_fusion), calls=%async_computation.1 | async-start | bytes 8388608 | tf_op jit(solution)/shard_map/all_to_all | solution.py:39
